TPU v7x, 128 devices: a whole 4x4x4 slice. The times are simulated.
128 devices in a mesh: rel: 4 (over z), ent: 32 (over y, x, core).
Axes of the slice: x: 4, y: 4, z: 4, core: 2. Of those that a mesh axis runs over, the one named last changes fastest.
Arguments:
- features: bfloat16 [16384, 512], P('ent'), may hold values from -6 to 6
- w_self: bfloat16 [512, 512], replicated, may hold values from -0.25 to 0.25
- basis_mats: bfloat16 [16384, 512], replicated, may hold values from -0.046875 to 0.046875
- basis_coeffs: float32 [1000, 32], replicated, may hold values from -5 to 5
- group_rels: int32 [1000], P('rel'), may hold values from 0 to 999, each once
- rel_local: int32 [65536], P(('rel', 'ent')), may hold values from 0 to 249
- edge_src: int32 [65536], P(('rel', 'ent')), may hold values from 0 to 16383, as said below
- edge_dst: int32 [65536], P(('rel', 'ent')), may hold values from 0 to 16383, as said below
- block_counts: int32 [4, 32, 32], P('rel', 'ent'), may hold values from 1 to 16, as said below
- cotangent: bfloat16 [16384, 512], P('ent'), may hold values from -6 to 6
Outputs:
- activations: bfloat16 [16384, 512], P('ent')
- grad_features: bfloat16 [16384, 512], P('ent')
- grad_basis: float32 [16384, 512], P(('rel', 'ent'))
Inputs may be any that keep to these rules, and one draw needn't show every extreme that they name: `edge_src`: slot i's source is owned by ent index (i // 512) % 32: it lies in [that index * 512, that index * 512 + 512). `edge_dst`: slot i's destination is owned by block index k = (i % 512) // 16: it lies in [k * 512, k * 512 + 512); within each aligned block of 16 slots the destinations are non-decreasing; the live slots of a block are its first block_counts ones. `block_counts`: one relation group, drawn from the seed, has every block full.
All inputs are finite; a program needn't handle non-finite values.
Results may differ from a plain program's by a relative error of at most 0.0059.
Values may be sent and summed in bfloat16 or wider, within the bound.
A program may use at most 192 MiB of HBM per device.

v0:
```python
import jax
import jax.numpy as jnp
from jax import lax
from jax.sharding import PartitionSpec as P

BF = jnp.bfloat16
F32 = jnp.float32


def dot(a, b, dims=((1,), (0,)), precision=None):
    return lax.dot_general(a, b, (dims, ((), ())), preferred_element_type=F32, precision=precision)


def swap(x, axis):
    return lax.all_to_all(x, axis, split_axis=0, concat_axis=0, tiled=True)


def per_device(
    features,
    w_self,
    basis_mats,
    basis_coeffs,
    group_rels,
    rel_local,
    edge_src,
    edge_dst,
    block_counts,
    cotangent,
):
    n_ent, width = features.shape
    ent_count = lax.axis_size("ent")
    rel_count = lax.axis_size("rel")
    slots = rel_local.shape[0]
    cap = slots // ent_count
    bases = basis_coeffs.shape[1]
    rels = basis_coeffs.shape[0]
    part = width // rel_count
    q = lax.axis_index("rel")
    s = lax.axis_index("ent")
    all_slots = slots * rel_count
    pos = jnp.arange(slots, dtype=jnp.int32)
    limits = jnp.repeat(block_counts.reshape(ent_count), cap, total_repeat_length=slots)
    live = pos % cap < limits
    src_own = edge_src - s * n_ent
    dst_own = jnp.where(live, edge_dst - pos // cap * n_ent, n_ent)
    rel_own = group_rels[rel_local]
    meta = jnp.stack([src_own, dst_own, rel_own])
    meta = lax.all_gather(meta, "rel").reshape(rel_count, 3, ent_count, cap)
    meta = meta.transpose(2, 1, 0, 3)
    src = meta[:, 0].reshape(all_slots)
    arrived = swap(meta[:, 1:], "ent")
    dst = arrived[:, 0].reshape(all_slots)
    rel = arrived[:, 1].reshape(all_slots)
    ids = jnp.arange(n_ent, dtype=jnp.int32)[:, None]
    pick_src = (ids == src[None, :]).astype(BF)
    feat_part = lax.dynamic_slice_in_dim(features, q * part, part, 1)
    rows = dot(pick_src, feat_part, ((0,), (0,))).astype(BF)
    rows = swap(rows.reshape(ent_count, rel_count * cap, part), "ent").reshape(all_slots, part)
    pick_rel = (jnp.arange(rels, dtype=jnp.int32)[:, None] == rel[None, :]).astype(F32)
    coef_t = dot(basis_coeffs, pick_rel, ((0,), (0,)), lax.Precision.HIGHEST)
    pick = (ids == dst[None, :]).astype(BF)
    degree = jnp.sum(pick, axis=1, dtype=F32)
    inverse = (1.0 / jnp.maximum(degree, 1.0))[:, None]
    mixed_t = (
        (coef_t[:, None, :] * rows.T.astype(F32)[None]).reshape(bases * part, all_slots).astype(BF)
    )
    agg = dot(pick, mixed_t, ((1,), (1,))).astype(BF)
    basis_part = lax.dynamic_slice_in_dim(
        basis_mats.reshape(bases, width, width), q * part, part, 1
    ).reshape(bases * part, width)
    partial = dot(agg, basis_part).astype(BF)
    partial = swap(partial.reshape(n_ent, rel_count, part).transpose(1, 0, 2), "rel")
    sums = jnp.sum(partial.astype(F32), axis=0)
    w_part = lax.dynamic_slice_in_dim(w_self, q * part, part, 1)
    cot = lax.dynamic_slice_in_dim(cotangent, q * part, part, 1).astype(F32)
    pre = dot(features, w_part) + sums * inverse
    sig = jax.nn.sigmoid(pre)
    act = (pre * sig).astype(BF)
    grad_pre = (cot * (sig * (1.0 + pre * (1.0 - sig)))).astype(BF)
    act = lax.all_gather(act, "rel", axis=1, tiled=True)
    grad_pre = lax.all_gather(grad_pre, "rel", axis=1, tiled=True)
    scaled = (grad_pre.astype(F32) * inverse).astype(BF)
    basis_terms = dot(agg, scaled, ((0,), (0,))).astype(BF)
    basis_terms = swap(basis_terms.reshape(ent_count, part, width), "ent")
    block = jnp.sum(basis_terms.astype(F32), axis=0)
    per_rel = bases // rel_count
    routes = [
        (r * ent_count + b, b // per_rel * ent_count + b % per_rel * rel_count + r)
        for r in range(rel_count)
        for b in range(bases)
    ]
    grad_basis = lax.ppermute(block, ("rel", "ent"), routes)
    back_t = dot(basis_part, scaled, ((1,), (1,))).astype(BF)
    spread = dot(back_t, pick).reshape(bases, part, all_slots)
    grad_rows = jnp.sum(spread * coef_t[:, None, :], axis=0).astype(BF).T
    grad_rows = swap(grad_rows.reshape(ent_count, rel_count * cap, part), "ent")
    w_rows = lax.dynamic_slice_in_dim(w_self, q * part, part, 0)
    grad_part = dot(grad_pre, w_rows, ((1,), (1,))) + dot(
        pick_src, grad_rows.reshape(all_slots, part)
    )
    grad_features = lax.all_gather(grad_part.astype(BF), "rel", axis=1, tiled=True)
    return (act, grad_features, grad_basis)


def solution(mesh):
    placed = (
        P("ent", None),
        P(),
        P(),
        P(),
        P("rel"),
        P(("rel", "ent")),
        P(("rel", "ent")),
        P(("rel", "ent")),
        P("rel", "ent", None),
        P("ent", None),
    )
    return jax.shard_map(
        per_device,
        mesh=mesh,
        in_specs=placed,
        out_specs=(P("ent", None), P("ent", None), P(("rel", "ent"), None)),
        check_vma=False,
    )
```

profile of v0, /device:TPU:27, one launch (start us, length us, event | category | flops | bytes accessed | tf_op | source)
XLA Modules:
  0.0 229.3 jit_solution(15646126451064702323)
XLA Ops:
  0.7 1.8 fusion.33
  2.5 2.1 fusion.32
  6.0 4.5 %compare_select_fusion.1 = (s32[512,1]{0,1:T(1,128)S(1)}, s32[512,1]{0,1:T(1,128)S(1)}) fusion(s32[]{:T(128)} %bitcast.31, s32[]{:T(128)} %bitcast.32, s32[]{:T(128)} %bitcast.33, s32[]{:T(128)} %bitcast.34, s32[]{:T(128)} %bitcast.35, s32[]{:T(128)} %bitcast.37, s32[]{:T(128)} %bitcast.36, s32[512,1]{0,1:T(1,128)S(1)} %bitcast.106, s32[512,1]{0,1:T(1,128)S(1)} %bitcast.105), kind=kLoop, calls=%fused_computation.66 | loop fusion | flops 7168 | bytes 8220 | tf_op jit(solution)/shard_map/jit(_take)/gather | solution.py:42
  11.4 3.6 %gather_fusion = s32[512]{0:T(512)S(1)} fusion(s32[250]{0:T(256)} %param.16, s32[1024]{0:T(1024)S(1)} %pad_clamp_fusion), kind=kCustom, calls=%fused_computation | custom fusion | bytes 6144 | tf_op jit(solution)/shard_map/gather | solution.py:46
  15.0 16.4 %fusion.23 = s32[512]{0:T(512)S(1)} fusion(s32[512]{0:T(512)} %param.19, pred[512]{0:T(512)(128)(4,1)S(1)} %get-tuple-element.51, pred[512]{0:T(512)(128)(4,1)S(1)} %get-tuple-element.50, pred[512]{0:T(512)(128)(4,1)S(1)} %get-tuple-element.49, pred[512]{0:T(512)(128)(4,1)S(1)} %get-tuple-element.48, pred[512]{0:T(512)(128)(4,1)S(1)} %get-tuple-element.47, ...), kind=kLoop, calls=%fused_computation.85 | loop fusion | flops 25600 | bytes 21108 | tf_op jit(solution)/shard_map/jit(_where)/select_n | solution.py:45
  31.4 10.5 %all-gather.1 = s32[4,3,512]{2,1,0:T(4,128)S(1)} all-gather(s32[1,3,512]{2,1,0:T(4,128)S(1)} %add_bitcast_fusion), channel_id=2, replica_groups=mesh['rel'=4,'ent'=32] {'rel'}, dimensions={0}, use_global_device_ids=true | all-gather | bytes 30720 | tf_op jit(solution)/shard_map/all_gather | solution.py:48
  42.9 10.3 %all-to-all-start = ((s32[32,1,128]{2,1,0:T(1,128)}), s32[32,1,128]{2,1,0:T(1,128)S(1)}, u32[]{:S(2)}, u32[]{:S(2)}) async-start(s32[32,1,128]{2,1,0:T(1,128)} %reshape.365), calls=%async_computation | async-start | bytes 32768 | tf_op jit(solution)/shard_map/all_to_all | solution.py:15
  53.3 2.1 fusion.6
  55.4 1.9 all-to-all-done
  57.3 7.0 %all-to-all-start.1 = ((bf16[32,64,128]{2,1,0:T(8,128)(2,1)}), bf16[32,64,128]{2,1,0:T(8,128)(2,1)S(1)}, u32[]{:S(2)}, u32[]{:S(2)}) async-start(bf16[32,64,128]{2,1,0:T(8,128)(2,1)} %bitcast.44), calls=%async_computation.1 | async-start | bytes 1048576 | tf_op jit(solution)/shard_map/all_to_all | solution.py:15
  64.3 4.6 %constant_dynamic-slice_fusion.1 = bf16[32,128,512]{2,1,0:T(8,128)(2,1)} fusion(bf16[32,512,512]{2,1,0:T(8,128)(2,1)} %bitcast.98, s32[]{:T(128)S(6)} %select_n.47), kind=kLoop, calls=%fused_computation.95 | loop fusion | bytes 8388612 | tf_op jit(solution)/shard_map/dynamic_slice | solution.py:68
  70.5 3.0 %fusion.7 = f32[32,2048]{1,0:T(8,128)S(1)} fusion(f32[1000,32]{0,1:T(8,128)S(1)} %copy-done.4, s32[2048]{0:T(1024)S(1)} %eq.52), kind=kOutput, calls=%fused_computation.18 | convolution fusion | flops 788480000 | bytes 398336 | tf_op jit(solution)/shard_map/dot_general | solution.py:11
  73.9 6.8 %multiply_convert_fusion = bf16[32,128,2048]{2,1,0:T(8,128)(2,1)} fusion(f32[128,2048]{1,0:T(8,128)S(1)} %bitcast.93, f32[32,2048]{1,0:T(8,128)S(1)} %fusion.7), kind=kLoop, calls=%fused_computation.2 | loop fusion | flops 16777216 | bytes 18087936 | tf_op jit(solution)/shard_map/convert_element_type | solution.py:65
  80.8 13.9 %convolution_convert_fusion = bf16[512,4096]{1,0:T(8,128)(2,1)} fusion(bf16[4096,2048]{1,0:T(8,128)(2,1)} %bitcast.92, s32[2048]{0:T(1024)S(1)} %eq.48), kind=kOutput, calls=%fused_computation.6 | convolution fusion | flops 8593080320 | bytes 20979712 | tf_op jit(solution)/shard_map/dot_general | solution.py:11
  94.7 5.5 %convolution_convert_fusion.3 = bf16[512,512]{0,1:T(8,128)(2,1)} fusion(bf16[512,4096]{1,0:T(8,128)(2,1)} %convolution_convert_fusion, bf16[4096,512]{1,0:T(8,128)(2,1)S(1)} %bitcast.95), kind=kOutput, calls=%fused_computation.23 | convolution fusion | flops 2147745792 | bytes 8912896 | tf_op jit(solution)/shard_map/dot_general | solution.py:11
  100.1 3.8 %all-to-all-start.2 = ((bf16[4,512,128]{1,2,0:T(8,128)(2,1)}), bf16[4,512,128]{1,2,0:T(8,128)(2,1)S(1)}, u32[]{:S(2)}, u32[]{:S(2)}) async-start(bf16[4,512,128]{1,2,0:T(8,128)(2,1)} %bitcast.51), calls=%async_computation.2 | async-start | bytes 1048576 | tf_op jit(solution)/shard_map/all_to_all | solution.py:15
  105.5 7.4 %all-to-all-done.2 = bf16[4,512,128]{1,2,0:T(8,128)(2,1)S(1)} async-done(((bf16[4,512,128]{1,2,0:T(8,128)(2,1)}), bf16[4,512,128]{1,2,0:T(8,128)(2,1)S(1)}, u32[]{:S(2)}, u32[]{:S(2)}) %all-to-all-start.2) | async-done | bytes 524320 | tf_op jit(solution)/shard_map/all_to_all | solution.py:15
  113.4 10.7 %all_gather.18 = bf16[512,512]{0,1:T(8,128)(2,1)S(1)} all-gather(bf16[512,128]{0,1:T(8,128)(2,1)S(1)} %get-tuple-element.54), channel_id=1, replica_groups=mesh['rel'=4,'ent'=32] {'rel'}, dimensions={1}, use_global_device_ids=true | all-gather | bytes 655360 | tf_op jit(solution)/shard_map/all_gather | solution.py:81
  124.1 6.6 %convolution_convert_fusion.1 = bf16[4096,512]{1,0:T(8,128)(2,1)} fusion(bf16[512,4096]{1,0:T(8,128)(2,1)} %convolution_convert_fusion, bf16[512,512]{0,1:T(8,128)(2,1)S(1)} %all_gather.18, f32[512]{0:T(512)S(1)} %maximum_divide_fusion), kind=kOutput, calls=%fused_computation.7 | convolution fusion | flops 2150367232 | bytes 8914944 | tf_op jit(solution)/shard_map/dot_general | solution.py:11
  130.8 11.3 %all-to-all-start.4 = ((bf16[32,128,512]{2,1,0:T(8,128)(2,1)}), bf16[32,128,512]{2,1,0:T(8,128)(2,1)}, u32[]{:S(2)}, u32[]{:S(2)}) async-start(bf16[32,128,512]{2,1,0:T(8,128)(2,1)} %bitcast.96), calls=%async_computation.4 | async-start | bytes 8388608 | tf_op jit(solution)/shard_map/all_to_all | solution.py:15
  142.1 11.1 %all_gather.17 = bf16[512,512]{0,1:T(8,128)(2,1)S(1)} all-gather(bf16[512,128]{0,1:T(8,128)(2,1)S(1)} %get-tuple-element.55), channel_id=1, replica_groups=mesh['rel'=4,'ent'=32] {'rel'}, dimensions={1}, use_global_device_ids=true | all-gather | bytes 655360 | tf_op jit(solution)/shard_map/all_gather | solution.py:80
  153.2 1.0 copy.35
  154.2 4.5 %convolution_convert_fusion.2.clone.5 = bf16[4096,512]{1,0:T(8,128)(2,1)S(1)} fusion(bf16[4096,512]{1,0:T(8,128)(2,1)} %bitcast.94, bf16[512,512]{0,1:T(8,128)(2,1)S(1)} %all_gather.18, f32[512]{0:T(512)S(1)} %maximum_divide_fusion), kind=kOutput, calls=%fused_computation.8.clone.clone.clone.2 | convolution fusion | flops 2150367232 | bytes 8914944 | tf_op jit(solution)/shard_map/dot_general | solution.py:11
  158.7 14.6 %fusion.3 = f32[4096,2048]{1,0:T(8,128)} fusion(s32[2048]{0:T(1024)S(1)} %eq.48, bf16[4096,512]{1,0:T(8,128)(2,1)S(1)} %convolution_convert_fusion.2.clone.5), kind=kOutput, calls=%fused_computation.14 | convolution fusion | flops 8590983168 | bytes 37756928 | tf_op jit(solution)/shard_map/dot_general | solution.py:11
  173.3 12.5 %multiply_reduce_fusion = bf16[128,2048]{1,0:T(8,128)(2,1)S(1)} fusion(f32[32,128,2048]{2,1,0:T(8,128)} %bitcast.91, f32[32,2048]{1,0:T(8,128)S(1)} %fusion.7), kind=kLoop, calls=%fused_computation.1 | loop fusion | flops 16515072 | bytes 34340864 | tf_op jit(solution)/shard_map/reduce_sum | solution.py:95
  185.8 1.0 copy.34
  186.8 5.1 %all-to-all-done.4 = bf16[32,128,512]{2,1,0:T(8,128)(2,1)} async-done(((bf16[32,128,512]{2,1,0:T(8,128)(2,1)}), bf16[32,128,512]{2,1,0:T(8,128)(2,1)}, u32[]{:S(2)}, u32[]{:S(2)}) %all-to-all-start.4) | async-done | bytes 4194336 | tf_op jit(solution)/shard_map/all_to_all | solution.py:15
  191.9 7.6 %all-to-all-start.3 = ((bf16[32,64,128]{2,1,0:T(8,128)(2,1)}), bf16[32,64,128]{2,1,0:T(8,128)(2,1)S(1)}, u32[]{:S(2)}, u32[]{:S(2)}) async-start(bf16[32,64,128]{2,1,0:T(8,128)(2,1)} %bitcast.54), calls=%async_computation.3 | async-start | bytes 1048576 | tf_op jit(solution)/shard_map/all_to_all | solution.py:15
  199.9 2.8 %convert_reduce_fusion = f32[128,512]{1,0:T(8,128)S(1)} fusion(bf16[32,128,512]{2,1,0:T(8,128)(2,1)} %all-to-all-done.4), kind=kLoop, calls=%fused_computation.3 | loop fusion | flops 4128768 | bytes 4456448 | tf_op jit(solution)/shard_map/reduce_sum | solution.py:85
  202.7 4.7 %collective-permute-start = (f32[128,512]{1,0:T(8,128)S(1)}, f32[128,512]{1,0:T(8,128)S(1)}, u32[]{:S(2)}, u32[]{:S(2)}) collective-permute-start(f32[128,512]{1,0:T(8,128)S(1)} %convert_reduce_fusion), channel_id=1, source_target_pairs={{0,0},{1,4},{2,8},{3,12},{4,16},{5,20},{6,24},{7,28},{8,32},{9,36}... | collective-permute-start | bytes 786440 | tf_op jit(solution)/shard_map/ppermute | solution.py:92
  207.4 1.2 all-to-all-done.3
  209.5 18.3 %all_gather.19 = bf16[512,512]{1,0:T(8,128)(2,1)S(1)} all-gather(bf16[512,128]{1,0:T(8,128)(2,1)S(1)} %fusion.14), channel_id=1, replica_groups=mesh['rel'=4,'ent'=32] {'rel'}, dimensions={1}, use_global_device_ids=true | all-gather | bytes 655360 | tf_op jit(solution)/shard_map/all_gather | solution.py:101
  (45 shorter events, 10.2 us)
Async XLA Ops:
  0.6 52.7 %copy-start = (bf16[512,512]{1,0:T(8,128)(2,1)S(1)}, bf16[512,512]{1,0:T(8,128)(2,1)}, u32[]{:S(2)}) copy-start(bf16[512,512]{1,0:T(8,128)(2,1)} %param.12) | copy-start | bytes 1572868
  42.9 14.5 %all-to-all-start = ((s32[32,1,128]{2,1,0:T(1,128)}), s32[32,1,128]{2,1,0:T(1,128)S(1)}, u32[]{:S(2)}, u32[]{:S(2)}) async-start(s32[32,1,128]{2,1,0:T(1,128)} %reshape.365), calls=%async_computation | async-start | bytes 32768 | tf_op jit(solution)/shard_map/all_to_all | solution.py:15
  57.3 16.1 %all-to-all-start.1 = ((bf16[32,64,128]{2,1,0:T(8,128)(2,1)}), bf16[32,64,128]{2,1,0:T(8,128)(2,1)S(1)}, u32[]{:S(2)}, u32[]{:S(2)}) async-start(bf16[32,64,128]{2,1,0:T(8,128)(2,1)} %bitcast.44), calls=%async_computation.1 | async-start | bytes 1048576 | tf_op jit(solution)/shard_map/all_to_all | solution.py:15
  64.3 6.2 %copy-start.4 = (f32[1000,32]{0,1:T(8,128)S(1)}, f32[1000,32]{0,1:T(8,128)}, u32[]{:S(2)}) copy-start(f32[1000,32]{0,1:T(8,128)} %param.15) | copy-start | bytes 384004
  80.7 13.9 %copy-start.2 = (bf16[32,128,512]{2,1,0:T(8,128)(2,1)S(1)}, bf16[32,128,512]{2,1,0:T(8,128)(2,1)}, u32[]{:S(2)}) copy-start(bf16[32,128,512]{2,1,0:T(8,128)(2,1)} %constant_dynamic-slice_fusion.1) | copy-start | bytes 12582916
  94.7 18.3 %copy-start.3 = (bf16[512,512]{1,0:T(8,128)(2,1)S(1)}, bf16[512,512]{1,0:T(8,128)(2,1)}, u32[]{:S(2)}) copy-start(bf16[512,512]{1,0:T(8,128)(2,1)} %param.13) | copy-start | bytes 1572868
  100.1 12.8 %all-to-all-start.2 = ((bf16[4,512,128]{1,2,0:T(8,128)(2,1)}), bf16[4,512,128]{1,2,0:T(8,128)(2,1)S(1)}, u32[]{:S(2)}, u32[]{:S(2)}) async-start(bf16[4,512,128]{1,2,0:T(8,128)(2,1)} %bitcast.51), calls=%async_computation.2 | async-start | bytes 1048576 | tf_op jit(solution)/shard_map/all_to_all | solution.py:15
  130.8 61.1 %all-to-all-start.4 = ((bf16[32,128,512]{2,1,0:T(8,128)(2,1)}), bf16[32,128,512]{2,1,0:T(8,128)(2,1)}, u32[]{:S(2)}, u32[]{:S(2)}) async-start(bf16[32,128,512]{2,1,0:T(8,128)(2,1)} %bitcast.96), calls=%async_computation.4 | async-start | bytes 8388608 | tf_op jit(solution)/shard_map/all_to_all | solution.py:15
  191.9 16.7 %all-to-all-start.3 = ((bf16[32,64,128]{2,1,0:T(8,128)(2,1)}), bf16[32,64,128]{2,1,0:T(8,128)(2,1)S(1)}, u32[]{:S(2)}, u32[]{:S(2)}) async-start(bf16[32,64,128]{2,1,0:T(8,128)(2,1)} %bitcast.54), calls=%async_computation.3 | async-start | bytes 1048576 | tf_op jit(solution)/shard_map/all_to_all | solution.py:15
  199.5 29.8 %copy-start.1 = (bf16[512,512]{1,0:T(8,128)(2,1)S(1)}, bf16[512,512]{1,0:T(8,128)(2,1)}, u32[]{:S(2)}) copy-start(bf16[512,512]{1,0:T(8,128)(2,1)} %param.12) | copy-start | bytes 1572868
  202.7 25.1 %collective-permute-start = (f32[128,512]{1,0:T(8,128)S(1)}, f32[128,512]{1,0:T(8,128)S(1)}, u32[]{:S(2)}, u32[]{:S(2)}) collective-permute-start(f32[128,512]{1,0:T(8,128)S(1)} %convert_reduce_fusion), channel_id=1, source_target_pairs={{0,0},{1,4},{2,8},{3,12},{4,16},{5,20},{6,24},{7,28},{8,32},{9,36}... | collective-permute-start | bytes 786440 | tf_op jit(solution)/shard_map/ppermute | solution.py:92
where the time goes:
time: 230 us; the launch traced here: 229 us
  matrix products  51.8 us (23%)
  blocking collectives  50.6 us (22%)
  other arithmetic  46.6 us (20%)
  starting transfers between devices  44.7 us (19%)
  local copies, waits for them, and re-layouts  19 us (8%)
  waiting for transfers between devices  15.7 us (7%)
    dot_general x10, matrix products, dot(): lax.dot_general(a, b, (dims, ((), ())), preferred_element_type=F32, preci...  51.8 us
    all_to_all x5, starting transfers between devices, swap(): return lax.all_to_all(x, axis, split_axis=0, concat_axis=0, tiled=True)  40 us
    all_gather x1, blocking collectives, per_device(): lax.all_gather(grad_part.astype(BF), 'rel', axis=1, tiled=True)  18.3 us
    select_n x1, other arithmetic, per_device(): dst_own = jnp.where(live, edge_dst - pos // cap * n_ent, n_ent)  16.4 us
    all_to_all x5, waiting for transfers between devices, swap(): return lax.all_to_all(x, axis, split_axis=0, concat_axis=0, tiled=True)  15.7 us
    reduce_sum x1, other arithmetic, per_device(): grad_rows = jnp.sum(spread * coef_t[:, None, :], axis=0).astype(BF).T  12.5 us
    all_gather x1, blocking collectives, per_device(): act = lax.all_gather(act, 'rel', axis=1, tiled=True)  11.1 us
    all_gather x1, blocking collectives, per_device(): grad_pre = lax.all_gather(grad_pre, 'rel', axis=1, tiled=True)  10.7 us
  transfers between devices with their start and end apart: 6, of which 4 were waited for; matrix products, arithmetic and copies ran while one was open for 22% of the time, Pallas kernels for 0%

commit v1 on v0

--- a/solution.py
+++ b/solution.py
@@ -5,6 +5,15 @@
 
 BF = jnp.bfloat16
 F32 = jnp.float32
+
+
+def _see_meshes(vals, arr):
+    even = jnp.split(
+        lax.all_gather(jnp.concatenate([vals, arr], 0), "rel", axis=1, tiled=True),
+        [vals.shape[0]],
+        0,
+    )
+    return even
 
 
 def dot(a, b, dims=((1,), (0,)), precision=None):
@@ -77,8 +86,7 @@
     sig = jax.nn.sigmoid(pre)
     act = (pre * sig).astype(BF)
     grad_pre = (cot * (sig * (1.0 + pre * (1.0 - sig)))).astype(BF)
-    act = lax.all_gather(act, "rel", axis=1, tiled=True)
-    grad_pre = lax.all_gather(grad_pre, "rel", axis=1, tiled=True)
+    act, grad_pre = _see_meshes(act, grad_pre)
     scaled = (grad_pre.astype(F32) * inverse).astype(BF)
     basis_terms = dot(agg, scaled, ((0,), (0,))).astype(BF)
     basis_terms = swap(basis_terms.reshape(ent_count, part, width), "ent")

time: 230 us -> 252 us (1.096)
  waiting for transfers between devices: 15.7 us -> 49.8 us
  blocking collectives: 50.6 us -> 28.7 us
  between operations: 0.92 us -> 14.3 us
  matrix products: 51.8 us -> 48.3 us
    all_gather x0 -> x1, waiting for transfers between devices: none -> 23.5 us  [_see_meshes(): lax.all_gather(jnp.concatenate([vals, arr], 0), 'rel', axis=1, tiled=True)]
    all_gather x2 -> x0, blocking collectives: 21.8 us -> none  [the longest x1 11.1 us: per_device(): act = lax.all_gather(act, 'rel', axis=1, tiled=True)]
    all_to_all x5, waiting for transfers between devices: 15.7 us -> 26.3 us  [swap(): return lax.all_to_all(x, axis, split_axis=0, concat_axis=0, tiled=True)]
    dot_general x10, matrix products: 51.8 us -> 48.3 us  [dot(): lax.dot_general(a, b, (dims, ((), ())), preferred_element_type=F32, preci...]
  transfers between devices with their start and end apart: 6 -> 7, of which waited for: 4 -> 5; matrix products, arithmetic and copies ran while one was open for 22% -> 20% of each run, Pallas kernels for 0% -> 0%
where the time goes in v1:
time: 252 us; the launch traced here: 250 us
  waiting for transfers between devices  49.8 us (20%)
  matrix products  48.3 us (19%)
  other arithmetic  47.3 us (19%)
  starting transfers between devices  42.7 us (17%)
  blocking collectives  28.7 us (11%)
  local copies, waits for them, and re-layouts  19 us (8%)
  between operations  14.3 us (6%)
    dot_general x10, matrix products, dot(): lax.dot_general(a, b, (dims, ((), ())), preferred_element_type=F32, preci...  48.3 us
    all_to_all x5, starting transfers between devices, swap(): return lax.all_to_all(x, axis, split_axis=0, concat_axis=0, tiled=True)  37.5 us
    all_to_all x5, waiting for transfers between devices, swap(): return lax.all_to_all(x, axis, split_axis=0, concat_axis=0, tiled=True)  26.3 us
    all_gather x1, waiting for transfers between devices, _see_meshes(): lax.all_gather(jnp.concatenate([vals, arr], 0), 'rel', axis=1, tiled=True)  23.5 us
    all_gather x1, blocking collectives, per_device(): lax.all_gather(grad_part.astype(BF), 'rel', axis=1, tiled=True)  18.2 us
    select_n x1, other arithmetic, per_device(): dst_own = jnp.where(live, edge_dst - pos // cap * n_ent, n_ent)  16.4 us
    reduce_sum x1, other arithmetic, per_device(): grad_rows = jnp.sum(spread * coef_t[:, None, :], axis=0).astype(BF).T  12.5 us
    all_gather x1, blocking collectives, per_device(): meta = lax.all_gather(meta, 'rel').reshape(rel_count, 3, ent_count, cap)  10.5 us
  transfers between devices with their start and end apart: 7, of which 5 were waited for; matrix products, arithmetic and copies ran while one was open for 20% of the time, Pallas kernels for 0%

profile of v1, /device:TPU:27, one launch (start us, length us, event | category | flops | bytes accessed | tf_op | source)
XLA Modules:
  0.0 250.2 jit_solution(15186833405366950322)
XLA Ops:
  7.2 1.8 fusion.34
  9.0 2.1 fusion.33
  12.6 4.5 %compare_select_fusion.1 = (s32[512,1]{0,1:T(1,128)S(1)}, s32[512,1]{0,1:T(1,128)S(1)}) fusion(s32[]{:T(128)} %bitcast.31, s32[]{:T(128)} %bitcast.32, s32[]{:T(128)} %bitcast.33, s32[]{:T(128)} %bitcast.34, s32[]{:T(128)} %bitcast.35, s32[]{:T(128)} %bitcast.37, s32[]{:T(128)} %bitcast.36, s32[512,1]{0,1:T(1,128)S(1)} %bitcast.105, s32[512,1]{0,1:T(1,128)S(1)} %bitcast.104), kind=kLoop, calls=%fused_computation.68 | loop fusion | flops 7168 | bytes 8220 | tf_op jit(solution)/shard_map/jit(_take)/gather | solution.py:51
  17.9 3.6 %gather_fusion = s32[512]{0:T(512)S(1)} fusion(s32[250]{0:T(256)} %param.16, s32[1024]{0:T(1024)S(1)} %pad_clamp_fusion), kind=kCustom, calls=%fused_computation | custom fusion | bytes 6144 | tf_op jit(solution)/shard_map/gather | solution.py:55
  21.5 16.4 %fusion.24 = s32[512]{0:T(512)S(1)} fusion(s32[512]{0:T(512)} %param.19, pred[512]{0:T(512)(128)(4,1)S(1)} %get-tuple-element.51, pred[512]{0:T(512)(128)(4,1)S(1)} %get-tuple-element.50, pred[512]{0:T(512)(128)(4,1)S(1)} %get-tuple-element.49, pred[512]{0:T(512)(128)(4,1)S(1)} %get-tuple-element.48, pred[512]{0:T(512)(128)(4,1)S(1)} %get-tuple-element.47, ...), kind=kLoop, calls=%fused_computation.87 | loop fusion | flops 25600 | bytes 21108 | tf_op jit(solution)/shard_map/jit(_where)/select_n | solution.py:54
  37.9 10.5 %all-gather.1 = s32[4,3,512]{2,1,0:T(4,128)S(1)} all-gather(s32[1,3,512]{2,1,0:T(4,128)S(1)} %add_bitcast_fusion), channel_id=2, replica_groups=mesh['rel'=4,'ent'=32] {'rel'}, dimensions={0}, use_global_device_ids=true | all-gather | bytes 30720 | tf_op jit(solution)/shard_map/all_gather | solution.py:57
  49.4 10.3 %all-to-all-start = ((s32[32,1,128]{2,1,0:T(1,128)}), s32[32,1,128]{2,1,0:T(1,128)S(1)}, u32[]{:S(2)}, u32[]{:S(2)}) async-start(s32[32,1,128]{2,1,0:T(1,128)} %reshape.365), calls=%async_computation | async-start | bytes 32768 | tf_op jit(solution)/shard_map/all_to_all | solution.py:24
  59.8 2.1 fusion.6
  61.9 1.9 all-to-all-done
  63.9 7.0 %all-to-all-start.1 = ((bf16[32,64,128]{2,1,0:T(8,128)(2,1)}), bf16[32,64,128]{2,1,0:T(8,128)(2,1)S(1)}, u32[]{:S(2)}, u32[]{:S(2)}) async-start(bf16[32,64,128]{2,1,0:T(8,128)(2,1)} %bitcast.44), calls=%async_computation.1 | async-start | bytes 1048576 | tf_op jit(solution)/shard_map/all_to_all | solution.py:24
  70.9 4.6 %constant_dynamic-slice_fusion.1 = bf16[32,128,512]{2,1,0:T(8,128)(2,1)} fusion(bf16[32,512,512]{2,1,0:T(8,128)(2,1)} %bitcast.97, s32[]{:T(128)S(6)} %select_n.47), kind=kLoop, calls=%fused_computation.97 | loop fusion | bytes 8388612 | tf_op jit(solution)/shard_map/dynamic_slice | solution.py:77
  77.0 2.9 %fusion.7 = f32[32,2048]{1,0:T(8,128)S(1)} fusion(f32[1000,32]{0,1:T(8,128)S(1)} %copy-done.5, s32[2048]{0:T(1024)S(1)} %eq.52), kind=kOutput, calls=%fused_computation.18 | convolution fusion | flops 788480000 | bytes 398336 | tf_op jit(solution)/shard_map/dot_general | solution.py:20
  80.5 6.8 %multiply_convert_fusion = bf16[32,128,2048]{2,1,0:T(8,128)(2,1)} fusion(f32[128,2048]{1,0:T(8,128)S(1)} %bitcast.92, f32[32,2048]{1,0:T(8,128)S(1)} %fusion.7), kind=kLoop, calls=%fused_computation.2 | loop fusion | flops 16777216 | bytes 18087936 | tf_op jit(solution)/shard_map/convert_element_type | solution.py:74
  87.3 12.6 %convolution_convert_fusion = bf16[512,4096]{1,0:T(8,128)(2,1)S(1)} fusion(bf16[4096,2048]{1,0:T(8,128)(2,1)} %bitcast.91, s32[2048]{0:T(1024)S(1)} %eq.48), kind=kOutput, calls=%fused_computation.6 | convolution fusion | flops 8593080320 | bytes 20979712 | tf_op jit(solution)/shard_map/dot_general | solution.py:20
  99.9 3.2 %convolution_convert_fusion.3 = bf16[512,512]{0,1:T(8,128)(2,1)} fusion(bf16[512,4096]{1,0:T(8,128)(2,1)S(1)} %convolution_convert_fusion, bf16[4096,512]{1,0:T(8,128)(2,1)S(1)} %bitcast.94), kind=kOutput, calls=%fused_computation.23 | convolution fusion | flops 2147745792 | bytes 8912896 | tf_op jit(solution)/shard_map/dot_general | solution.py:20
  103.1 3.9 %all-to-all-start.2 = ((bf16[4,512,128]{1,2,0:T(8,128)(2,1)}), bf16[4,512,128]{1,2,0:T(8,128)(2,1)S(1)}, u32[]{:S(2)}, u32[]{:S(2)}) async-start(bf16[4,512,128]{1,2,0:T(8,128)(2,1)} %bitcast.51), calls=%async_computation.2 | async-start | bytes 1048576 | tf_op jit(solution)/shard_map/all_to_all | solution.py:24
  107.0 0.9 constant_dynamic-slice_fusion
  108.5 7.4 %all-to-all-done.2 = bf16[4,512,128]{1,2,0:T(8,128)(2,1)S(1)} async-done(((bf16[4,512,128]{1,2,0:T(8,128)(2,1)}), bf16[4,512,128]{1,2,0:T(8,128)(2,1)S(1)}, u32[]{:S(2)}, u32[]{:S(2)}) %all-to-all-start.2) | async-done | bytes 524320 | tf_op jit(solution)/shard_map/all_to_all | solution.py:24
  117.1 23.5 %all-gather.4.cloned.1.call-done = bf16[1024,512]{0,1:T(8,128)(2,1)} async-done(((bf16[1024,128]{0,1:T(8,128)(2,1)}), bf16[1024,512]{0,1:T(8,128)(2,1)}) %all-gather.4.cloned.1.call-update) | async-done | bytes 1048592 | tf_op jit(solution)/shard_map/all_gather | solution.py:12
  140.7 6.8 %convolution_convert_fusion.1 = bf16[4096,512]{1,0:T(8,128)(2,1)} fusion(bf16[512,4096]{1,0:T(8,128)(2,1)} %copy-done.6, f32[512]{0:T(512)S(1)} %maximum_divide_fusion, bf16[1024,512]{0,1:T(8,128)(2,1)} %all-gather.4.cloned.1.call-done), kind=kOutput, calls=%fused_computation.7 | convolution fusion | flops 2150367232 | bytes 8914944 | tf_op jit(solution)/shard_map/dot_general | solution.py:20
  147.4 8.8 %all-to-all-start.4 = ((bf16[32,128,512]{2,1,0:T(8,128)(2,1)}), bf16[32,128,512]{2,1,0:T(8,128)(2,1)}, u32[]{:S(2)}, u32[]{:S(2)}) async-start(bf16[32,128,512]{2,1,0:T(8,128)(2,1)} %bitcast.95), calls=%async_computation.4 | async-start | bytes 8388608 | tf_op jit(solution)/shard_map/all_to_all | solution.py:24
  156.3 1.0 copy.35
  157.3 4.5 %convolution_convert_fusion.2.clone.5 = bf16[4096,512]{1,0:T(8,128)(2,1)S(1)} fusion(bf16[4096,512]{1,0:T(8,128)(2,1)} %bitcast.93, f32[512]{0:T(512)S(1)} %maximum_divide_fusion, bf16[1024,512]{0,1:T(8,128)(2,1)S(1)} %copy-done.3), kind=kOutput, calls=%fused_computation.8.clone.clone.clone.2 | convolution fusion | flops 2150367232 | bytes 8914944 | tf_op jit(solution)/shard_map/dot_general | solution.py:20
  161.8 14.6 %fusion.3 = f32[4096,2048]{1,0:T(8,128)} fusion(s32[2048]{0:T(1024)S(1)} %eq.48, bf16[4096,512]{1,0:T(8,128)(2,1)S(1)} %convolution_convert_fusion.2.clone.5), kind=kOutput, calls=%fused_computation.14 | convolution fusion | flops 8590983168 | bytes 37756928 | tf_op jit(solution)/shard_map/dot_general | solution.py:20
  176.4 12.5 %multiply_reduce_fusion = bf16[128,2048]{1,0:T(8,128)(2,1)S(1)} fusion(f32[32,128,2048]{2,1,0:T(8,128)} %bitcast.90, f32[32,2048]{1,0:T(8,128)S(1)} %fusion.7), kind=kLoop, calls=%fused_computation.1 | loop fusion | flops 16515072 | bytes 34340864 | tf_op jit(solution)/shard_map/reduce_sum | solution.py:103
  188.9 1.0 copy.34
  189.9 16.2 %all-to-all-done.4 = bf16[32,128,512]{2,1,0:T(8,128)(2,1)} async-done(((bf16[32,128,512]{2,1,0:T(8,128)(2,1)}), bf16[32,128,512]{2,1,0:T(8,128)(2,1)}, u32[]{:S(2)}, u32[]{:S(2)}) %all-to-all-start.4) | async-done | bytes 4194336 | tf_op jit(solution)/shard_map/all_to_all | solution.py:24
  206.1 7.6 %all-to-all-start.3 = ((bf16[32,64,128]{2,1,0:T(8,128)(2,1)}), bf16[32,64,128]{2,1,0:T(8,128)(2,1)S(1)}, u32[]{:S(2)}, u32[]{:S(2)}) async-start(bf16[32,64,128]{2,1,0:T(8,128)(2,1)} %bitcast.54), calls=%async_computation.3 | async-start | bytes 1048576 | tf_op jit(solution)/shard_map/all_to_all | solution.py:24
  214.0 2.8 %convert_reduce_fusion = f32[128,512]{1,0:T(8,128)S(1)} fusion(bf16[32,128,512]{2,1,0:T(8,128)(2,1)} %all-to-all-done.4), kind=kLoop, calls=%fused_computation.3 | loop fusion | flops 4128768 | bytes 4456448 | tf_op jit(solution)/shard_map/reduce_sum | solution.py:93
  216.8 5.2 %collective-permute-start = (f32[128,512]{1,0:T(8,128)S(1)}, f32[128,512]{1,0:T(8,128)S(1)}, u32[]{:S(2)}, u32[]{:S(2)}) collective-permute-start(f32[128,512]{1,0:T(8,128)S(1)} %convert_reduce_fusion), channel_id=1, source_target_pairs={{0,0},{1,4},{2,8},{3,12},{4,16},{5,20},{6,24},{7,28},{8,32},{9,36}... | collective-permute-start | bytes 786440 | tf_op jit(solution)/shard_map/ppermute | solution.py:100
  222.8 0.9 fusion.14
  223.7 18.2 %all_gather.15 = bf16[512,512]{1,0:T(8,128)(2,1)S(1)} all-gather(bf16[512,128]{1,0:T(8,128)(2,1)S(1)} %fusion.14), channel_id=1, replica_groups=mesh['rel'=4,'ent'=32] {'rel'}, dimensions={1}, use_global_device_ids=true | all-gather | bytes 655360 | tf_op jit(solution)/shard_map/all_gather | solution.py:109
  (53 shorter events, 9.9 us)
Async XLA Ops:
  7.2 52.7 %copy-start = (bf16[512,512]{1,0:T(8,128)(2,1)S(1)}, bf16[512,512]{1,0:T(8,128)(2,1)}, u32[]{:S(2)}) copy-start(bf16[512,512]{1,0:T(8,128)(2,1)} %param.12) | copy-start | bytes 1572868
  49.4 14.5 %all-to-all-start = ((s32[32,1,128]{2,1,0:T(1,128)}), s32[32,1,128]{2,1,0:T(1,128)S(1)}, u32[]{:S(2)}, u32[]{:S(2)}) async-start(s32[32,1,128]{2,1,0:T(1,128)} %reshape.365), calls=%async_computation | async-start | bytes 32768 | tf_op jit(solution)/shard_map/all_to_all | solution.py:24
  63.9 16.1 %all-to-all-start.1 = ((bf16[32,64,128]{2,1,0:T(8,128)(2,1)}), bf16[32,64,128]{2,1,0:T(8,128)(2,1)S(1)}, u32[]{:S(2)}, u32[]{:S(2)}) async-start(bf16[32,64,128]{2,1,0:T(8,128)(2,1)} %bitcast.44), calls=%async_computation.1 | async-start | bytes 1048576 | tf_op jit(solution)/shard_map/all_to_all | solution.py:24
  70.8 6.2 %copy-start.5 = (f32[1000,32]{0,1:T(8,128)S(1)}, f32[1000,32]{0,1:T(8,128)}, u32[]{:S(2)}) copy-start(f32[1000,32]{0,1:T(8,128)} %param.15) | copy-start | bytes 384004
  87.3 12.6 %copy-start.2 = (bf16[32,128,512]{2,1,0:T(8,128)(2,1)S(1)}, bf16[32,128,512]{2,1,0:T(8,128)(2,1)}, u32[]{:S(2)}) copy-start(bf16[32,128,512]{2,1,0:T(8,128)(2,1)} %constant_dynamic-slice_fusion.1) | copy-start | bytes 12582916
  99.9 3.2 %copy-start.6 = (bf16[512,4096]{1,0:T(8,128)(2,1)}, bf16[512,4096]{1,0:T(8,128)(2,1)S(1)}, u32[]{:S(2)}) copy-start(bf16[512,4096]{1,0:T(8,128)(2,1)S(1)} %convolution_convert_fusion) | copy-start | bytes 12582916
  99.9 16.0 %copy-start.4 = (bf16[512,512]{1,0:T(8,128)(2,1)S(1)}, bf16[512,512]{1,0:T(8,128)(2,1)}, u32[]{:S(2)}) copy-start(bf16[512,512]{1,0:T(8,128)(2,1)} %param.13) | copy-start | bytes 1572868
  103.1 12.8 %all-to-all-start.2 = ((bf16[4,512,128]{1,2,0:T(8,128)(2,1)}), bf16[4,512,128]{1,2,0:T(8,128)(2,1)S(1)}, u32[]{:S(2)}, u32[]{:S(2)}) async-start(bf16[4,512,128]{1,2,0:T(8,128)(2,1)} %bitcast.51), calls=%async_computation.2 | async-start | bytes 1048576 | tf_op jit(solution)/shard_map/all_to_all | solution.py:24
  106.9 33.7 %all-gather.4.cloned.1.call-start = ((), (), s32[]{:S(2)}) async-start(), calls=%async_computation.5 | async-start | bytes 1310720 | tf_op jit(solution)/shard_map/all_gather | solution.py:12
  147.4 8.8 %slice-start = ((bf16[1024,512]{0,1:T(8,128)(2,1)}), bf16[512,512]{0,1:T(8,128)(2,1)S(1)}, s32[]{:S(2)}) async-start(bf16[1024,512]{0,1:T(8,128)(2,1)} %all-gather.4.cloned.1.call-done), calls=%async_computation.6 | async-start | bytes 1048576 | tf_op jit(solution)/shard_map/split | solution.py:11
  147.4 9.8 %copy-start.3 = (bf16[1024,512]{0,1:T(8,128)(2,1)S(1)}, bf16[1024,512]{0,1:T(8,128)(2,1)}, u32[]{:S(2)}) copy-start(bf16[1024,512]{0,1:T(8,128)(2,1)} %all-gather.4.cloned.1.call-done) | copy-start | bytes 3145732
  147.4 58.7 %all-to-all-start.4 = ((bf16[32,128,512]{2,1,0:T(8,128)(2,1)}), bf16[32,128,512]{2,1,0:T(8,128)(2,1)}, u32[]{:S(2)}, u32[]{:S(2)}) async-start(bf16[32,128,512]{2,1,0:T(8,128)(2,1)} %bitcast.95), calls=%async_computation.4 | async-start | bytes 8388608 | tf_op jit(solution)/shard_map/all_to_all | solution.py:24
  206.1 16.7 %all-to-all-start.3 = ((bf16[32,64,128]{2,1,0:T(8,128)(2,1)}), bf16[32,64,128]{2,1,0:T(8,128)(2,1)S(1)}, u32[]{:S(2)}, u32[]{:S(2)}) async-start(bf16[32,64,128]{2,1,0:T(8,128)(2,1)} %bitcast.54), calls=%async_computation.3 | async-start | bytes 1048576 | tf_op jit(solution)/shard_map/all_to_all | solution.py:24
  213.7 29.7 %copy-start.1 = (bf16[512,512]{1,0:T(8,128)(2,1)S(1)}, bf16[512,512]{1,0:T(8,128)(2,1)}, u32[]{:S(2)}) copy-start(bf16[512,512]{1,0:T(8,128)(2,1)} %param.12) | copy-start | bytes 1572868
  216.8 25.0 %collective-permute-start = (f32[128,512]{1,0:T(8,128)S(1)}, f32[128,512]{1,0:T(8,128)S(1)}, u32[]{:S(2)}, u32[]{:S(2)}) collective-permute-start(f32[128,512]{1,0:T(8,128)S(1)} %convert_reduce_fusion), channel_id=1, source_target_pairs={{0,0},{1,4},{2,8},{3,12},{4,16},{5,20},{6,24},{7,28},{8,32},{9,36}... | collective-permute-start | bytes 786440 | tf_op jit(solution)/shard_map/ppermute | solution.py:100
Sparse Core Ops, SparseCore 0:
  117.3 23.3 all-gather.3
